TPU v7x, 512 devices: a whole 4x4x16 slice. The times are simulated.
512 devices in a mesh: dp: 16 (over x, y), mp: 32 (over z, core).
Axes of the slice: x: 4, y: 4, z: 16, core: 2. Of those that a mesh axis runs over, the one named last changes fastest.
Arguments:
- hidden_policy: bfloat16 [256, 16, 2048], P('dp', None, 'mp'), may hold values from -6 to 6
- hidden_reference: bfloat16 [256, 16, 2048], P('dp', None, 'mp'), may hold values from -6 to 6
- ffn_gain_policy: float32 [2048], replicated, may hold values from 0.1 to 1.9
- ffn_gain_reference: float32 [2048], replicated, may hold values from 0.1 to 1.9
- up_policy: bfloat16 [2048, 4096], P(None, 'mp'), may hold values from -0.125 to 0.125
- up_reference: bfloat16 [2048, 4096], P(None, 'mp'), may hold values from -0.125 to 0.125
- down_policy: bfloat16 [4096, 2048], P('mp'), may hold values from -0.1875 to 0.1875
- down_reference: bfloat16 [4096, 2048], P('mp'), may hold values from -0.1875 to 0.1875
- final_gain_policy: float32 [2048], replicated, may hold values from 0.1 to 1.9
- final_gain_reference: float32 [2048], replicated, may hold values from 0.1 to 1.9
- out_policy: bfloat16 [2048, 28672], P('dp', 'mp'), may hold values from -4 to 4
- out_reference: bfloat16 [2048, 28672], P('dp', 'mp'), may hold values from -4 to 4
- move_plan: int32 [256], replicated, may hold values from 0 to 255, as said below
- lengths: int32 [256], P('dp'), may hold values from 1 to 16, 2048 in all
- targets: int32 [256, 16], P('dp'), may hold values from 0 to 28671
Outputs:
- token_diff: float32 [256, 16], P('dp')
- seq_diff: float32 [256], P('dp')
Inputs may be any that keep to these rules, and one draw needn't show every extreme that they name: `move_plan`: A permutation of the slots; slot // 16 is the owning index of dp, each owning exactly 16 requests; from one index of dp to one owner go either no requests or exactly 2.
All inputs are finite; a program needn't handle non-finite values. No bound on the sum of `lengths` on one device may be relied on, other than what follows from the above.
Results may differ from a plain program's by a relative error of at most 0.0081.
Values may be sent and summed in bfloat16 or wider, within the bound.
A program may use at most 64 MiB of HBM per device.

v0:
```python
import jax
import jax.numpy as jnp
from jax import lax
from jax.sharding import PartitionSpec as P

D = 2048
epsilon = 1e-05


def select_rows(selector, values):
    return jnp.dot(selector, values, preferred_element_type=jnp.float32).astype(jnp.bfloat16)


def norm_from_sums(values, first_sum, second_sum, gain, width):
    center = first_sum / width
    spread = second_sum / width - center * center
    return (values - center[:, None]) * lax.rsqrt(spread + epsilon)[:, None] * gain


def local(
    hidden_policy,
    hidden_reference,
    ffn_gain_policy,
    ffn_gain_reference,
    up_policy,
    up_reference,
    down_policy,
    down_reference,
    final_gain_policy,
    final_gain_reference,
    out_policy,
    out_reference,
    move_plan,
    lengths,
    targets,
):
    dp_count = lax.axis_size("dp")
    dp_index = lax.axis_index("dp")
    mp_index = lax.axis_index("mp")
    req_count = hidden_policy.shape[0]
    slot_count = hidden_policy.shape[1]
    width_part = hidden_policy.shape[2]
    tokens_here = req_count * slot_count
    capacity = max(2, req_count // min(8, dp_count))
    buffer_slots = dp_count * capacity
    plan = move_plan.reshape(dp_count, req_count)
    owner_device = plan // req_count
    positions = jnp.arange(req_count, dtype=jnp.int32)
    earlier = positions[None, :] < positions[:, None]
    same_owner = owner_device[:, :, None] == owner_device[:, None, :]
    rank = jnp.sum(jnp.logical_and(same_owner, earlier[None]), axis=2)
    own_owner = lax.dynamic_index_in_dim(owner_device, dp_index, 0, keepdims=False)
    own_rank = lax.dynamic_index_in_dim(rank, dp_index, 0, keepdims=False)
    send_slot = own_owner * capacity + own_rank
    send_select = (jnp.arange(buffer_slots, dtype=jnp.int32)[:, None] == send_slot[None, :]).astype(
        jnp.bfloat16
    )
    packed = (
        select_rows(send_select, hidden_policy.reshape(req_count, slot_count * width_part)),
        select_rows(send_select, hidden_reference.reshape(req_count, slot_count * width_part)),
    )
    arrived = (
        lax.all_to_all(packed[0], "dp", split_axis=0, concat_axis=0, tiled=True),
        lax.all_to_all(packed[1], "dp", split_axis=0, concat_axis=0, tiled=True),
    )
    column = jnp.arange(dp_count, dtype=jnp.int32)[:, None] * capacity + rank
    local_row = plan - dp_index * req_count
    owned = owner_device == dp_index
    row_hot = jnp.logical_and(
        local_row.reshape(-1)[:, None] == positions[None, :], owned.reshape(-1)[:, None]
    ).astype(jnp.bfloat16)
    column_hot = (
        column.reshape(-1)[:, None] == jnp.arange(buffer_slots, dtype=jnp.int32)[None, :]
    ).astype(jnp.bfloat16)
    receive_select = jnp.dot(row_hot.T, column_hot, preferred_element_type=jnp.float32).astype(
        jnp.bfloat16
    )
    moved_policy = select_rows(receive_select, arrived[0]).reshape(tokens_here, width_part)
    moved_reference = select_rows(receive_select, arrived[1]).reshape(tokens_here, width_part)
    stream_policy = moved_policy.astype(jnp.float32)
    stream_reference = moved_reference.astype(jnp.float32)
    ffn_sums = lax.psum(
        (
            jnp.sum(stream_policy, axis=1),
            jnp.sum(stream_policy * stream_policy, axis=1),
            jnp.sum(stream_reference, axis=1),
            jnp.sum(stream_reference * stream_reference, axis=1),
        ),
        "mp",
    )
    gain_policy_part = lax.dynamic_slice_in_dim(ffn_gain_policy, mp_index * width_part, width_part)
    gain_reference_part = lax.dynamic_slice_in_dim(
        ffn_gain_reference, mp_index * width_part, width_part
    )
    normed_policy = norm_from_sums(
        stream_policy, ffn_sums[0], ffn_sums[1], gain_policy_part, D
    ).astype(jnp.bfloat16)
    normed_reference = norm_from_sums(
        stream_reference, ffn_sums[2], ffn_sums[3], gain_reference_part, D
    ).astype(jnp.bfloat16)
    pieces = (
        lax.all_gather(normed_policy, "mp", axis=1, tiled=True),
        lax.all_gather(normed_reference, "mp", axis=1, tiled=True),
    )
    pre_policy = jnp.dot(pieces[0], up_policy, preferred_element_type=jnp.float32)
    pre_reference = jnp.dot(pieces[1], up_reference, preferred_element_type=jnp.float32)
    units_policy = jax.nn.gelu(pre_policy).astype(jnp.bfloat16)
    units_reference = jax.nn.gelu(pre_reference).astype(jnp.bfloat16)
    terms = (
        jnp.dot(units_policy, down_policy, preferred_element_type=jnp.float32),
        jnp.dot(units_reference, down_reference, preferred_element_type=jnp.float32),
    )
    summed = (
        lax.psum_scatter(terms[0], "mp", scatter_dimension=1, tiled=True),
        lax.psum_scatter(terms[1], "mp", scatter_dimension=1, tiled=True),
    )
    after_policy = stream_policy + summed[0]
    after_reference = stream_reference + summed[1]
    final_sums = lax.psum(
        (
            jnp.sum(after_policy, axis=1),
            jnp.sum(after_policy * after_policy, axis=1),
            jnp.sum(after_reference, axis=1),
            jnp.sum(after_reference * after_reference, axis=1),
        ),
        "mp",
    )
    final_policy_part = lax.dynamic_slice_in_dim(
        final_gain_policy, mp_index * width_part, width_part
    )
    final_reference_part = lax.dynamic_slice_in_dim(
        final_gain_reference, mp_index * width_part, width_part
    )
    out_normed_policy = norm_from_sums(
        after_policy, final_sums[0], final_sums[1], final_policy_part, D
    ).astype(jnp.bfloat16)
    out_normed_reference = norm_from_sums(
        after_reference, final_sums[2], final_sums[3], final_reference_part, D
    ).astype(jnp.bfloat16)
    full_policy, full_reference = (
        lax.all_gather(out_normed_policy, "mp", axis=1, tiled=True),
        lax.all_gather(out_normed_reference, "mp", axis=1, tiled=True),
    )
    vocab_part = out_policy.shape[1]
    pieces = (
        lax.all_gather(out_policy, "dp", axis=0, tiled=True),
        lax.all_gather(out_reference, "dp", axis=0, tiled=True),
    )
    logits_policy = jnp.dot(full_policy, pieces[0], preferred_element_type=jnp.float32)
    logits_reference = jnp.dot(full_reference, pieces[1], preferred_element_type=jnp.float32)
    wanted = targets.reshape(tokens_here)
    entry_ids = jnp.arange(vocab_part, dtype=jnp.int32)[None, :] + mp_index * vocab_part
    target_hit = entry_ids == wanted[:, None]
    picked_policy = jnp.sum(jnp.where(target_hit, logits_policy, 0.0), axis=1)
    picked_reference = jnp.sum(jnp.where(target_hit, logits_reference, 0.0), axis=1)
    top_policy, top_reference = lax.pmax(
        (jnp.max(logits_policy, axis=1), jnp.max(logits_reference, axis=1)), "mp"
    )
    totals = lax.psum(
        (
            jnp.sum(jnp.exp(logits_policy - top_policy[:, None]), axis=1),
            jnp.sum(jnp.exp(logits_reference - top_reference[:, None]), axis=1),
            picked_policy,
            picked_reference,
        ),
        "mp",
    )
    logprob_policy = totals[2] - (top_policy + jnp.log(totals[0]))
    logprob_reference = totals[3] - (top_reference + jnp.log(totals[1]))
    live = jnp.arange(slot_count, dtype=jnp.int32)[None, :] < lengths[:, None]
    token_diff = jnp.where(
        live, (logprob_policy - logprob_reference).reshape(req_count, slot_count), jnp.float32(0.0)
    )
    seq_diff = jnp.sum(token_diff, axis=1)
    return (token_diff, seq_diff)


def solution(mesh):
    return jax.shard_map(
        local,
        mesh=mesh,
        in_specs=(
            P("dp", None, "mp"),
            P("dp", None, "mp"),
            P(),
            P(),
            P(None, "mp"),
            P(None, "mp"),
            P("mp", None),
            P("mp", None),
            P(),
            P(),
            P("dp", "mp"),
            P("dp", "mp"),
            P(),
            P("dp"),
            P("dp", None),
        ),
        out_specs=(P("dp", None), P("dp")),
        check_vma=False,
    )
```

profile of v0, /device:TPU:1, one launch (start us, length us, event | category | flops | bytes accessed | tf_op | source)
XLA Modules:
  0.0 811.6 jit_solution(14091598724623640920)
XLA Ops:
  8.0 0.8 reshape.153
  8.9 1.0 reshape.155
  11.1 7.6 all-to-all-start.1
  18.6 0.7 fusion.42
  20.2 1.0 reshape.154
  22.2 0.8 dynamic_slice.23
  23.0 2.2 all-to-all-done.1
  25.2 4.5 all-to-all-start
  30.0 6.2 all-to-all-done
  36.8 54.5 %all-reduce.2 = (f32[256]{0:T(256)S(1)}, f32[256]{0:T(256)S(1)}, f32[256]{0:T(256)S(1)}, f32[256]{0:T(256)S(1)}) all-reduce(f32[256]{0:T(256)S(1)} %get-tuple-element.46, f32[256]{0:T(256)S(1)} %get-tuple-element.47, f32[256]{0:T(256)S(1)} %get-tuple-element.7, f32[256]{0:T(256)S(1)} %get-tuple-element.6), channel_id=1, replica_groups=mesh['dp'=16,'mp'=32] {'mp'}, use_global_device_ids=true, to_apply=%region_19.20 | all-reduce | flops 1024 | bytes 8192 | tf_op jit(solution)/shard_map/psum | solution.py:82
  91.2 0.7 multiply_convert_fusion.1
  92.0 0.8 dynamic_slice.21
  93.6 63.8 %all-gather.13.cloned.1.call-done = bf16[256,2048]{0,1:T(8,128)(2,1)} async-done(((bf16[256,64]{0,1:T(8,128)(2,1)}), bf16[256,2048]{0,1:T(8,128)(2,1)}) %all-gather.13.cloned.1.call-update) | async-done | bytes 1048592 | tf_op jit(solution)/shard_map/all_gather | solution.py:103
  157.4 3.6 fusion.22
  161.1 66.3 %all-gather.7.cloned.1.call-done = bf16[256,2048]{0,1:T(8,128)(2,1)} async-done(((bf16[256,64]{0,1:T(8,128)(2,1)}), bf16[256,2048]{0,1:T(8,128)(2,1)}) %all-gather.7.cloned.1.call-update) | async-done | bytes 1048592 | tf_op jit(solution)/shard_map/all_gather | solution.py:102
  227.4 3.4 fusion.24
  231.5 0.8 dynamic_slice.24
  232.2 102.6 %reduce-scatter.5.cloned.1.call-done = f32[256,64]{0,1:T(8,128)} async-done(((f32[256,2048]{0,1:T(8,128)}), f32[256,64]{0,1:T(8,128)}) %reduce-scatter.5.cloned.1.call-update) | async-done | bytes 65552 | tf_op jit(solution)/shard_map/reduce_scatter | solution.py:115
  334.9 0.9 fusion.54
  335.7 109.6 %reduce-scatter.3.cloned.1.call-done = f32[256,64]{0,1:T(8,128)} async-done(((f32[256,2048]{0,1:T(8,128)}), f32[256,64]{0,1:T(8,128)}) %reduce-scatter.3.cloned.1.call-update) | async-done | bytes 65552 | tf_op jit(solution)/shard_map/reduce_scatter | solution.py:114
  445.4 0.9 fusion.53
  446.2 48.8 %all-reduce.1 = (f32[256]{0:T(256)S(1)}, f32[256]{0:T(256)S(1)}, f32[256]{0:T(256)S(1)}, f32[256]{0:T(256)S(1)}) all-reduce(f32[256]{0:T(256)S(1)} %get-tuple-element.13, f32[256]{0:T(256)S(1)} %get-tuple-element.12, f32[256]{0:T(256)S(1)} %get-tuple-element.11, f32[256]{0:T(256)S(1)} %get-tuple-element.10), channel_id=1, replica_groups=mesh['dp'=16,'mp'=32] {'mp'}, use_global_device_ids=true, to_apply=%region_24.25 | all-reduce | flops 1024 | bytes 8192 | tf_op jit(solution)/shard_map/psum | solution.py:119
  495.0 0.7 multiply_convert_fusion
  496.4 0.8 dynamic_slice.22
  498.0 69.6 %all-gather.15.cloned.1.call-done = bf16[256,2048]{0,1:T(8,128)(2,1)} async-done(((bf16[256,64]{0,1:T(8,128)(2,1)}), bf16[256,2048]{0,1:T(8,128)(2,1)}) %all-gather.15.cloned.1.call-update) | async-done | bytes 1048592 | tf_op jit(solution)/shard_map/all_gather | solution.py:142
  567.6 3.7 fusion.57
  571.3 60.5 %all-gather.11.cloned.1.call-done = bf16[2048,896]{1,0:T(8,128)(2,1)} async-done(((bf16[128,896]{1,0:T(8,128)(2,1)}), bf16[2048,896]{1,0:T(8,128)(2,1)}) %all-gather.11.cloned.1.call-update) | async-done | bytes 3670032 | tf_op jit(solution)/shard_map/all_gather | solution.py:146
  631.8 73.1 %all-gather.9.cloned.1.call-done = bf16[256,2048]{0,1:T(8,128)(2,1)} async-done(((bf16[256,64]{0,1:T(8,128)(2,1)}), bf16[256,2048]{0,1:T(8,128)(2,1)}) %all-gather.9.cloned.1.call-update) | async-done | bytes 1048592 | tf_op jit(solution)/shard_map/all_gather | solution.py:141
  704.9 3.7 fusion.58
  708.6 45.4 %all-reduce.3 = (f32[256]{0:T(256)S(1)}, f32[256]{0:T(256)S(1)}) all-reduce(f32[256]{0:T(256)S(1)} %get-tuple-element.42, f32[256]{0:T(256)S(1)} %get-tuple-element.44), channel_id=1, replica_groups=mesh['dp'=16,'mp'=32] {'mp'}, use_global_device_ids=true, to_apply=%region_28.29 | all-reduce | flops 512 | bytes 4096 | tf_op jit(solution)/shard_map/pmax | solution.py:156
  754.6 48.2 %all-reduce = (f32[256]{0:T(256)S(1)}, f32[256]{0:T(256)S(1)}, f32[256]{0:T(256)S(1)}, f32[256]{0:T(256)S(1)}) all-reduce(f32[256]{0:T(256)S(1)} %get-tuple-element.32, f32[256]{0:T(256)S(1)} %get-tuple-element.33, f32[256]{0:T(256)S(1)} %get-tuple-element.3, f32[256]{0:T(256)S(1)} %get-tuple-element.2), channel_id=1, replica_groups=mesh['dp'=16,'mp'=32] {'mp'}, use_global_device_ids=true, to_apply=%region_26.27 | all-reduce | flops 1024 | bytes 8192 | tf_op jit(solution)/shard_map/psum | solution.py:159
  802.9 1.3 fusion.55
  (60 shorter events, 7.8 us)
Async XLA Ops:
  8.0 149.4 %copy-start = (bf16[128,2048]{1,0:T(8,128)(2,1)S(1)}, bf16[128,2048]{1,0:T(8,128)(2,1)}, u32[]{:S(2)}) copy-start(bf16[128,2048]{1,0:T(8,128)(2,1)} %param.22) | copy-start | bytes 1572868
  11.1 14.1 %all-to-all-start.1 = ((bf16[16,2,1024]{2,1,0:T(2,128)(2,1)}), bf16[16,2,1024]{2,1,0:T(2,128)(2,1)S(1)}, u32[]{:S(2)}, u32[]{:S(2)}) async-start(bf16[16,2,1024]{2,1,0:T(2,128)(2,1)} %all_to_all.19), calls=%async_computation.2 | async-start | bytes 131072 | tf_op jit(solution)/shard_map/all_to_all | solution.py:64
  25.2 11.0 %all-to-all-start = ((bf16[16,2,1024]{2,1,0:T(2,128)(2,1)}), bf16[16,2,1024]{2,1,0:T(2,128)(2,1)S(1)}, u32[]{:S(2)}, u32[]{:S(2)}) async-start(bf16[16,2,1024]{2,1,0:T(2,128)(2,1)} %all_to_all.16), calls=%async_computation | async-start | bytes 131072 | tf_op jit(solution)/shard_map/all_to_all | solution.py:63
  29.7 127.7 %all-gather.13.cloned.1.call-start = ((), (), s32[]{:S(2)}) async-start(), calls=%async_computation.8 | async-start | bytes 1081344 | tf_op jit(solution)/shard_map/all_gather | solution.py:103
  36.4 190.9 %copy-start.1 = (bf16[128,2048]{1,0:T(8,128)(2,1)S(1)}, bf16[128,2048]{1,0:T(8,128)(2,1)}, u32[]{:S(2)}) copy-start(bf16[128,2048]{1,0:T(8,128)(2,1)} %param.21) | copy-start | bytes 1572868
  36.4 190.9 %copy-start.2 = (bf16[2048,128]{1,0:T(8,128)(2,1)S(1)}, bf16[2048,128]{1,0:T(8,128)(2,1)}, u32[]{:S(2)}) copy-start(bf16[2048,128]{1,0:T(8,128)(2,1)} %param.19) | copy-start | bytes 1572868
  92.0 135.4 %all-gather.7.cloned.1.call-start = ((), (), s32[]{:S(2)}) async-start(), calls=%async_computation.4 | async-start | bytes 1081344 | tf_op jit(solution)/shard_map/all_gather | solution.py:102
  93.6 241.3 %reduce-scatter.5.cloned.1.call-start = ((), (), s32[]{:S(2)}) async-start(), calls=%async_computation.9 | async-start | bytes 2162688 | tf_op jit(solution)/shard_map/reduce_scatter | solution.py:115
  161.0 336.8 %copy-start.3 = (s32[16,16]{1,0:T(8,128)S(1)}, s32[16,16]{1,0:T(8,128)}, u32[]{:S(2)}) copy-start(s32[16,16]{1,0:T(8,128)} %param.29) | copy-start | bytes 3076
  161.0 284.3 %reduce-scatter.3.cloned.1.call-start = ((), (), s32[]{:S(2)}) async-start(), calls=%async_computation.5 | async-start | bytes 2162688 | tf_op jit(solution)/shard_map/reduce_scatter | solution.py:114
  230.8 267.1 %all-gather.17.cloned.1.call-start = ((), (), s32[]{:S(2)}) async-start(), calls=%async_computation.11 | async-start | bytes 3899392 | tf_op jit(solution)/shard_map/all_gather | solution.py:147
  231.4 336.2 %all-gather.15.cloned.1.call-start = ((), (), s32[]{:S(2)}) async-start(), calls=%async_computation.10 | async-start | bytes 1081344 | tf_op jit(solution)/shard_map/all_gather | solution.py:142
  495.7 136.1 %all-gather.11.cloned.1.call-start = ((), (), s32[]{:S(2)}) async-start(), calls=%async_computation.7 | async-start | bytes 3899392 | tf_op jit(solution)/shard_map/all_gather | solution.py:146
  496.3 208.6 %all-gather.9.cloned.1.call-start = ((), (), s32[]{:S(2)}) async-start(), calls=%async_computation.6 | async-start | bytes 1081344 | tf_op jit(solution)/shard_map/all_gather | solution.py:141
  571.3 231.6 %copy-start.4 = (s32[16]{0:T(128)S(1)}, s32[16]{0:T(128)}, u32[]{:S(2)}) copy-start(s32[16]{0:T(128)} %param.28) | copy-start | bytes 196
Sparse Core Ops, SparseCore 0:
  92.1 65.2 all-gather.12
  159.5 67.8 all-gather.6
  230.2 104.6 reduce-scatter.4
  337.8 107.5 reduce-scatter.2
Sparse Core Ops, SparseCore 1:
  234.4 61.3 all-gather.16
  495.8 71.7 all-gather.14
  570.5 61.2 all-gather.10
  633.9 70.9 all-gather.8
where the time goes:
time: 812 us
  waiting for transfers between devices  555 us (68%)
  blocking collectives  197 us (24%)
  between operations  15.6 us (2%)
  matrix products  15.3 us (2%)
  starting transfers between devices  12.4 us (2%)
  other arithmetic  8.56 us (1%)
    reduce_scatter x1, waiting for transfers between devices, local(): lax.psum_scatter(terms[0], 'mp', scatter_dimension=1, tiled=True)  110 us
    reduce_scatter x1, waiting for transfers between devices, local(): lax.psum_scatter(terms[1], 'mp', scatter_dimension=1, tiled=True)  103 us
    all_gather x1, waiting for transfers between devices, local(): lax.all_gather(out_normed_policy, 'mp', axis=1, tiled=True)  73.1 us
    all_gather x1, waiting for transfers between devices, local(): lax.all_gather(out_normed_reference, 'mp', axis=1, tiled=True)  69.6 us
    all_gather x1, waiting for transfers between devices, local(): lax.all_gather(normed_policy, 'mp', axis=1, tiled=True)  66.3 us
    all_gather x1, waiting for transfers between devices, local(): lax.all_gather(normed_reference, 'mp', axis=1, tiled=True)  63.8 us
    all_gather x1, waiting for transfers between devices, local(): lax.all_gather(out_policy, 'dp', axis=0, tiled=True)  60.5 us
    psum x1, blocking collectives, local(): lax.psum((jnp.sum(stream_policy, axis=1), jnp.sum(stream_policy * stream_...  54.5 us
  transfers between devices with their start and end apart: 10, of which 9 were waited for; matrix products, arithmetic and copies ran while one was open for 3% of the time, Pallas kernels for 0%

commit v1 on v0

--- a/solution.py
+++ b/solution.py
@@ -5,6 +5,12 @@
 
 D = 2048
 epsilon = 1e-05
+drive_the_frames = lambda frame: jnp.concatenate(
+    jax.lax.all_to_all(
+        jnp.stack(jax.lax.axis_size("mp") * [frame], axis=0), "mp", concat_axis=0, split_axis=0
+    ),
+    1,
+)
 
 
 def select_rows(selector, values):
@@ -99,7 +105,7 @@
         stream_reference, ffn_sums[2], ffn_sums[3], gain_reference_part, D
     ).astype(jnp.bfloat16)
     pieces = (
-        lax.all_gather(normed_policy, "mp", axis=1, tiled=True),
+        drive_the_frames(normed_policy),
         lax.all_gather(normed_reference, "mp", axis=1, tiled=True),
     )
     pre_policy = jnp.dot(pieces[0], up_policy, preferred_element_type=jnp.float32)

time: 812 us -> 756 us (0.931)
  waiting for transfers between devices: 555 us -> 490 us
  starting transfers between devices: 12.4 us -> 21.6 us
    all_gather x1 -> x0, waiting for transfers between devices: 66.3 us -> none  [local(): lax.all_gather(normed_policy, 'mp', axis=1, tiled=True)]
    all_to_all x0 -> x1, starting transfers between devices: none -> 9.24 us  [jax.lax.all_to_all(jnp.stack(jax.lax.axis_size('mp') * [frame], axis=0),...]
  transfers between devices with their start and end apart: 10 -> 10, of which waited for: 9 -> 8; matrix products, arithmetic and copies ran while one was open for 3% -> 3% of each run, Pallas kernels for 0% -> 0%
where the time goes in v1:
time: 756 us; the launch traced here: 755 us
  waiting for transfers between devices  490 us (65%)
  blocking collectives  197 us (26%)
  starting transfers between devices  21.6 us (3%)
  between operations  15.7 us (2%)
  matrix products  14 us (2%)
  local copies, waits for them, and re-layouts  8.89 us (1%)
  other arithmetic  7.97 us (1%)
    reduce_scatter x1, waiting for transfers between devices, local(): lax.psum_scatter(terms[0], 'mp', scatter_dimension=1, tiled=True)  109 us
    reduce_scatter x1, waiting for transfers between devices, local(): lax.psum_scatter(terms[1], 'mp', scatter_dimension=1, tiled=True)  100 us
    all_gather x1, waiting for transfers between devices, local(): lax.all_gather(out_normed_policy, 'mp', axis=1, tiled=True)  73.1 us
    all_gather x1, waiting for transfers between devices, local(): lax.all_gather(out_normed_reference, 'mp', axis=1, tiled=True)  70 us
    all_gather x1, waiting for transfers between devices, local(): lax.all_gather(normed_reference, 'mp', axis=1, tiled=True)  67.2 us
    all_gather x1, waiting for transfers between devices, local(): lax.all_gather(out_policy, 'dp', axis=0, tiled=True)  60.5 us
    psum x1, blocking collectives, local(): lax.psum((jnp.sum(stream_policy, axis=1), jnp.sum(stream_policy * stream_...  54.5 us
    psum x1, blocking collectives, local(): lax.psum((jnp.sum(after_policy, axis=1), jnp.sum(after_policy * after_pol...  48.7 us
  transfers between devices with their start and end apart: 10, of which 8 were waited for; matrix products, arithmetic and copies ran while one was open for 3% of the time, Pallas kernels for 0%

profile of v1, /device:TPU:1, one launch (start us, length us, event | category | flops | bytes accessed | tf_op | source)
XLA Modules:
  0.0 754.9 jit_solution(3424842067668434724)
XLA Ops:
  8.0 0.8 reshape.183
  8.9 1.0 reshape.187
  11.1 7.6 %all-to-all-start.2 = ((bf16[16,2,1024]{2,1,0:T(2,128)(2,1)}), bf16[16,2,1024]{2,1,0:T(2,128)(2,1)S(1)}, u32[]{:S(2)}, u32[]{:S(2)}) async-start(bf16[16,2,1024]{2,1,0:T(2,128)(2,1)} %all_to_all.23), calls=%async_computation.3 | async-start | bytes 131072 | tf_op jit(solution)/shard_map/all_to_all | solution.py:70
  18.7 0.7 fusion.42
  20.2 1.0 reshape.184
  22.3 0.8 dynamic_slice.23
  23.1 2.2 all-to-all-done.2
  25.2 4.5 all-to-all-start
  30.0 6.2 all-to-all-done
  36.8 54.5 %all-reduce.2 = (f32[256]{0:T(256)S(1)}, f32[256]{0:T(256)S(1)}, f32[256]{0:T(256)S(1)}, f32[256]{0:T(256)S(1)}) all-reduce(f32[256]{0:T(256)S(1)} %get-tuple-element.46, f32[256]{0:T(256)S(1)} %get-tuple-element.47, f32[256]{0:T(256)S(1)} %get-tuple-element.7, f32[256]{0:T(256)S(1)} %get-tuple-element.6), channel_id=1, replica_groups=mesh['dp'=16,'mp'=32] {'mp'}, use_global_device_ids=true, to_apply=%region_19.20 | all-reduce | flops 1024 | bytes 8192 | tf_op jit(solution)/shard_map/psum | solution.py:88
  92.0 0.8 dynamic_slice.21
  92.9 1.1 stack.2
  94.0 9.2 %all-to-all-start.1 = ((bf16[32,256,64]{1,2,0:T(8,128)(2,1)}), bf16[32,256,64]{1,2,0:T(8,128)(2,1)S(1)}, u32[]{:S(2)}, u32[]{:S(2)}) async-start(bf16[32,256,64]{1,2,0:T(8,128)(2,1)} %stack.2), calls=%async_computation.1 | async-start | bytes 2097152 | tf_op jit(solution)/shard_map/all_to_all | solution.py:9
  103.4 67.2 %all-gather.10.cloned.1.call-done = bf16[256,2048]{0,1:T(8,128)(2,1)} async-done(((bf16[256,64]{0,1:T(8,128)(2,1)}), bf16[256,2048]{0,1:T(8,128)(2,1)}) %all-gather.10.cloned.1.call-update) | async-done | bytes 1048592 | tf_op jit(solution)/shard_map/all_gather | solution.py:109
  170.5 3.5 fusion.22
  174.1 2.2 fusion.24
  177.0 0.8 dynamic_slice.24
  177.8 100.3 %reduce-scatter.5.cloned.1.call-done = f32[256,64]{0,1:T(8,128)} async-done(((f32[256,2048]{0,1:T(8,128)}), f32[256,64]{0,1:T(8,128)}) %reduce-scatter.5.cloned.1.call-update) | async-done | bytes 65552 | tf_op jit(solution)/shard_map/reduce_scatter | solution.py:121
  278.0 0.9 fusion.54
  278.9 109.4 %reduce-scatter.3.cloned.1.call-done = f32[256,64]{0,1:T(8,128)} async-done(((f32[256,2048]{0,1:T(8,128)}), f32[256,64]{0,1:T(8,128)}) %reduce-scatter.3.cloned.1.call-update) | async-done | bytes 65552 | tf_op jit(solution)/shard_map/reduce_scatter | solution.py:120
  388.3 0.9 fusion.53
  389.1 48.7 %all-reduce.1 = (f32[256]{0:T(256)S(1)}, f32[256]{0:T(256)S(1)}, f32[256]{0:T(256)S(1)}, f32[256]{0:T(256)S(1)}) all-reduce(f32[256]{0:T(256)S(1)} %get-tuple-element.13, f32[256]{0:T(256)S(1)} %get-tuple-element.12, f32[256]{0:T(256)S(1)} %get-tuple-element.11, f32[256]{0:T(256)S(1)} %get-tuple-element.10), channel_id=1, replica_groups=mesh['dp'=16,'mp'=32] {'mp'}, use_global_device_ids=true, to_apply=%region_24.25 | all-reduce | flops 1024 | bytes 8192 | tf_op jit(solution)/shard_map/psum | solution.py:125
  437.9 0.7 multiply_convert_fusion
  439.2 0.8 dynamic_slice.22
  440.8 70.0 %all-gather.12.cloned.1.call-done = bf16[256,2048]{0,1:T(8,128)(2,1)} async-done(((bf16[256,64]{0,1:T(8,128)(2,1)}), bf16[256,2048]{0,1:T(8,128)(2,1)}) %all-gather.12.cloned.1.call-update) | async-done | bytes 1048592 | tf_op jit(solution)/shard_map/all_gather | solution.py:148
  510.8 3.7 fusion.57
  514.6 60.5 %all-gather.8.cloned.1.call-done = bf16[2048,896]{1,0:T(8,128)(2,1)} async-done(((bf16[128,896]{1,0:T(8,128)(2,1)}), bf16[2048,896]{1,0:T(8,128)(2,1)}) %all-gather.8.cloned.1.call-update) | async-done | bytes 3670032 | tf_op jit(solution)/shard_map/all_gather | solution.py:152
  575.1 73.1 %all-gather.6.cloned.1.call-done = bf16[256,2048]{0,1:T(8,128)(2,1)} async-done(((bf16[256,64]{0,1:T(8,128)(2,1)}), bf16[256,2048]{0,1:T(8,128)(2,1)}) %all-gather.6.cloned.1.call-update) | async-done | bytes 1048592 | tf_op jit(solution)/shard_map/all_gather | solution.py:147
  648.1 3.7 fusion.58
  651.9 45.4 %all-reduce.3 = (f32[256]{0:T(256)S(1)}, f32[256]{0:T(256)S(1)}) all-reduce(f32[256]{0:T(256)S(1)} %get-tuple-element.42, f32[256]{0:T(256)S(1)} %get-tuple-element.44), channel_id=1, replica_groups=mesh['dp'=16,'mp'=32] {'mp'}, use_global_device_ids=true, to_apply=%region_28.29 | all-reduce | flops 512 | bytes 4096 | tf_op jit(solution)/shard_map/pmax | solution.py:162
  697.9 48.2 %all-reduce = (f32[256]{0:T(256)S(1)}, f32[256]{0:T(256)S(1)}, f32[256]{0:T(256)S(1)}, f32[256]{0:T(256)S(1)}) all-reduce(f32[256]{0:T(256)S(1)} %get-tuple-element.32, f32[256]{0:T(256)S(1)} %get-tuple-element.33, f32[256]{0:T(256)S(1)} %get-tuple-element.3, f32[256]{0:T(256)S(1)} %get-tuple-element.2), channel_id=1, replica_groups=mesh['dp'=16,'mp'=32] {'mp'}, use_global_device_ids=true, to_apply=%region_26.27 | all-reduce | flops 1024 | bytes 8192 | tf_op jit(solution)/shard_map/psum | solution.py:165
  746.2 1.3 fusion.55
  (62 shorter events, 7.8 us)
Async XLA Ops:
  8.0 162.5 %copy-start = (bf16[128,2048]{1,0:T(8,128)(2,1)S(1)}, bf16[128,2048]{1,0:T(8,128)(2,1)}, u32[]{:S(2)}) copy-start(bf16[128,2048]{1,0:T(8,128)(2,1)} %param.22) | copy-start | bytes 1572868
  8.0 162.5 %copy-start.1 = (bf16[2048,128]{1,0:T(8,128)(2,1)S(1)}, bf16[2048,128]{1,0:T(8,128)(2,1)}, u32[]{:S(2)}) copy-start(bf16[2048,128]{1,0:T(8,128)(2,1)} %param.20) | copy-start | bytes 1572868
  11.1 14.1 %all-to-all-start.2 = ((bf16[16,2,1024]{2,1,0:T(2,128)(2,1)}), bf16[16,2,1024]{2,1,0:T(2,128)(2,1)S(1)}, u32[]{:S(2)}, u32[]{:S(2)}) async-start(bf16[16,2,1024]{2,1,0:T(2,128)(2,1)} %all_to_all.23), calls=%async_computation.3 | async-start | bytes 131072 | tf_op jit(solution)/shard_map/all_to_all | solution.py:70
  25.2 11.0 %all-to-all-start = ((bf16[16,2,1024]{2,1,0:T(2,128)(2,1)}), bf16[16,2,1024]{2,1,0:T(2,128)(2,1)S(1)}, u32[]{:S(2)}, u32[]{:S(2)}) async-start(bf16[16,2,1024]{2,1,0:T(2,128)(2,1)} %all_to_all.19), calls=%async_computation | async-start | bytes 131072 | tf_op jit(solution)/shard_map/all_to_all | solution.py:69
  29.7 140.8 %all-gather.10.cloned.1.call-start = ((), (), s32[]{:S(2)}) async-start(), calls=%async_computation.8 | async-start | bytes 1081344 | tf_op jit(solution)/shard_map/all_gather | solution.py:109
  94.0 80.0 %all-to-all-start.1 = ((bf16[32,256,64]{1,2,0:T(8,128)(2,1)}), bf16[32,256,64]{1,2,0:T(8,128)(2,1)S(1)}, u32[]{:S(2)}, u32[]{:S(2)}) async-start(bf16[32,256,64]{1,2,0:T(8,128)(2,1)} %stack.2), calls=%async_computation.1 | async-start | bytes 2097152 | tf_op jit(solution)/shard_map/all_to_all | solution.py:9
  103.3 70.8 %copy-start.2 = (bf16[128,2048]{1,0:T(8,128)(2,1)S(1)}, bf16[128,2048]{1,0:T(8,128)(2,1)}, u32[]{:S(2)}) copy-start(bf16[128,2048]{1,0:T(8,128)(2,1)} %param.21) | copy-start | bytes 1572868
  103.3 70.8 %copy-start.3 = (bf16[2048,128]{1,0:T(8,128)(2,1)S(1)}, bf16[2048,128]{1,0:T(8,128)(2,1)}, u32[]{:S(2)}) copy-start(bf16[2048,128]{1,0:T(8,128)(2,1)} %param.19) | copy-start | bytes 1572868
  103.3 174.7 %reduce-scatter.5.cloned.1.call-start = ((), (), s32[]{:S(2)}) async-start(), calls=%async_computation.9 | async-start | bytes 2162688 | tf_op jit(solution)/shard_map/reduce_scatter | solution.py:121
  174.0 214.2 %reduce-scatter.3.cloned.1.call-start = ((), (), s32[]{:S(2)}) async-start(), calls=%async_computation.5 | async-start | bytes 2162688 | tf_op jit(solution)/shard_map/reduce_scatter | solution.py:120
  174.1 266.6 %copy-start.4 = (s32[16,16]{1,0:T(8,128)S(1)}, s32[16,16]{1,0:T(8,128)}, u32[]{:S(2)}) copy-start(s32[16,16]{1,0:T(8,128)} %param.29) | copy-start | bytes 3076
  176.4 264.4 %all-gather.14.cloned.1.call-start = ((), (), s32[]{:S(2)}) async-start(), calls=%async_computation.11 | async-start | bytes 3899392 | tf_op jit(solution)/shard_map/all_gather | solution.py:153
  177.0 333.9 %all-gather.12.cloned.1.call-start = ((), (), s32[]{:S(2)}) async-start(), calls=%async_computation.10 | async-start | bytes 1081344 | tf_op jit(solution)/shard_map/all_gather | solution.py:148
  438.6 136.5 %all-gather.8.cloned.1.call-start = ((), (), s32[]{:S(2)}) async-start(), calls=%async_computation.7 | async-start | bytes 3899392 | tf_op jit(solution)/shard_map/all_gather | solution.py:152
  439.1 209.0 %all-gather.6.cloned.1.call-start = ((), (), s32[]{:S(2)}) async-start(), calls=%async_computation.6 | async-start | bytes 1081344 | tf_op jit(solution)/shard_map/all_gather | solution.py:147
  514.6 231.6 %copy-start.5 = (s32[16]{0:T(128)S(1)}, s32[16]{0:T(128)}, u32[]{:S(2)}) copy-start(s32[16]{0:T(128)} %param.28) | copy-start | bytes 196
Sparse Core Ops, SparseCore 0:
  92.1 78.3 all-gather.9
  174.1 103.8 reduce-scatter.4
  281.1 107.1 reduce-scatter.2
Sparse Core Ops, SparseCore 1:
  179.9 60.5 all-gather.13
  438.7 72.1 all-gather.11
  513.8 61.2 all-gather.7
  577.2 70.9 all-gather.5
